TPU v7x, 32 devices: a whole 2x2x4 slice. The times are simulated.
32 devices in a mesh: expert: 8 (over z, x), replica: 4 (over y, core).
Axes of the slice: x: 2, y: 2, z: 4, core: 2. Of those that a mesh axis runs over, the one named last changes fastest.
Arguments:
- tokens: bfloat16 [4096, 2048], P(('expert', 'replica')), may hold values from -6 to 6
- cotangent: bfloat16 [4096, 2048], P(('expert', 'replica')), may hold values from -6 to 6
- route_weights: float32 [4096, 8], P(('expert', 'replica')), may hold values from 0.02 to 0.4
- expert_ids: int32 [4096, 8], P(('expert', 'replica')), may hold values from 0 to 15, as said below
- slot_ids: int32 [4096, 8], P(('expert', 'replica')), may hold values from 0 to 63, as said below
- kept_mask: int32 [4096, 8], P(('expert', 'replica')), may hold values from 0 to 1, as said below
- gate_weight: bfloat16 [16, 2048, 384], P('expert'), may hold values from -0.125 to 0.125
- up_weight: bfloat16 [16, 2048, 384], P('expert'), may hold values from -0.125 to 0.125
- down_weight: bfloat16 [16, 384, 2048], P('expert'), may hold values from -0.3125 to 0.3125
- projector_basis: float32 [2048, 256], P('expert'), may hold values from -6 to 6
Outputs:
- token_grads: bfloat16 [4096, 2048], P(('expert', 'replica'))
- projected_grads: float32 [16, 3, 384, 256], P('expert')
- new_basis: float32 [2048, 256], P('expert')
Inputs may be any that keep to these rules, and one draw needn't show every extreme that they name: `expert_ids`: each row names 8 different experts. `slot_ids`: within one device's rows, the kept routes to one expert take slots 0, 1, 2, ... in the order of rows and then of the position in the row; a dropped route has slot 0; in every draw some expert receives 64 kept routes from every device's rows. `kept_mask`: a route is dropped exactly when 64 earlier routes of the same device's rows go to the same expert.
All inputs are finite; a program needn't handle non-finite values.
Results may differ from a plain program's by a relative error of at most 0.019.
Values may be sent and summed in bfloat16 or wider, within the bound.
A program may use at most 128 MiB of HBM per device.

v0:
```python
import math
import jax
import jax.numpy as jnp
from jax import lax
from jax.sharding import PartitionSpec as P


def body(
    tokens,
    cotangent,
    route_weights,
    expert_ids,
    slot_ids,
    kept_mask,
    gate_weight,
    up_weight,
    down_weight,
    projector_basis,
):
    tok_count, model_width = tokens.shape
    route_top = expert_ids.shape[1]
    local_count = gate_weight.shape[0]
    group_count = lax.axis_size("expert")
    expert_total = local_count * group_count
    slot_cap = tok_count * route_top // expert_total
    slot_total = expert_total * slot_cap
    route_count = tok_count * route_top
    target = jnp.where(kept_mask > 0, expert_ids * slot_cap + slot_ids, slot_total).reshape(-1)
    table = (
        jnp.full((slot_total,), route_count, jnp.int32)
        .at[target]
        .set(jnp.arange(route_count, dtype=jnp.int32), mode="drop")
    )
    owner = table // route_top
    tokens_pad = jnp.concatenate([tokens, jnp.zeros((1, model_width), tokens.dtype)], 0)
    cotangent_pad = jnp.concatenate([cotangent, jnp.zeros((1, model_width), cotangent.dtype)], 0)
    weight_pad = jnp.concatenate([route_weights.reshape(-1), jnp.zeros((1,), jnp.float32)], 0)
    x_send = tokens_pad[owner].reshape(group_count, local_count * slot_cap, model_width)
    dy_send = (cotangent_pad[owner].astype(jnp.float32) * weight_pad[table][:, None]).astype(
        jnp.bfloat16
    )
    dy_send = dy_send.reshape(group_count, local_count * slot_cap, model_width)
    full_basis = lax.all_gather(
        projector_basis.astype(jnp.bfloat16), "expert", axis=0, tiled=True
    ).astype(projector_basis.dtype)
    projector = (full_basis * (1.0 / math.sqrt(model_width))).astype(jnp.bfloat16)
    block_shape = (group_count, local_count, slot_cap, model_width)
    x_recv, dy_recv = (
        lax.all_to_all(x_send, "expert", split_axis=0, concat_axis=0, tiled=True),
        lax.all_to_all(dy_send, "expert", split_axis=0, concat_axis=0, tiled=True),
    )
    x_rows = x_recv.reshape(block_shape)
    gate = jnp.einsum("sjcd,jdf->sjcf", x_rows, gate_weight, preferred_element_type=jnp.float32)
    upper = jnp.einsum("sjcd,jdf->sjcf", x_rows, up_weight, preferred_element_type=jnp.float32)
    sigma = jax.nn.sigmoid(gate)
    activated = gate * sigma
    slope = sigma * (1.0 + gate * (1.0 - sigma))
    hidden = (activated * upper).astype(jnp.bfloat16)
    x_proj = jnp.einsum(
        "sjcd,dr->sjcr", x_rows, projector, preferred_element_type=jnp.float32
    ).astype(jnp.bfloat16)
    x_rows, upper, activated, slope, hidden, x_proj = (
        x_rows,
        upper,
        activated,
        slope,
        hidden,
        x_proj,
    )
    dy_rows = dy_recv.reshape(block_shape)
    hidden_grad = jnp.einsum(
        "sjcd,jfd->sjcf", dy_rows, down_weight, preferred_element_type=jnp.float32
    )
    up_grad = (hidden_grad * activated).astype(jnp.bfloat16)
    gate_grad = (hidden_grad * upper * slope).astype(jnp.bfloat16)
    row_grads = jnp.einsum(
        "sjcf,jdf->sjcd", gate_grad, gate_weight, preferred_element_type=jnp.float32
    )
    row_grads = row_grads + jnp.einsum(
        "sjcf,jdf->sjcd", up_grad, up_weight, preferred_element_type=jnp.float32
    )
    row_grads = row_grads.astype(jnp.bfloat16).reshape(
        group_count, local_count * slot_cap, model_width
    )
    returned = lax.all_to_all(row_grads, "expert", split_axis=0, concat_axis=0, tiled=True).reshape(
        slot_total, model_width
    )
    returned = jnp.concatenate([returned, jnp.zeros((1, model_width), jnp.bfloat16)], 0)
    token_grads = jnp.sum(
        returned[target].reshape(tok_count, route_top, model_width).astype(jnp.float32), axis=1
    ).astype(jnp.bfloat16)
    dy_proj = jnp.einsum(
        "sjcd,dr->sjcr", dy_rows, projector, preferred_element_type=jnp.float32
    ).astype(jnp.bfloat16)
    partial_grads = jnp.stack(
        [
            jnp.einsum("sjcf,sjcr->jfr", gate_grad, x_proj, preferred_element_type=jnp.float32),
            jnp.einsum("sjcf,sjcr->jfr", up_grad, x_proj, preferred_element_type=jnp.float32),
            jnp.einsum("sjcf,sjcr->jfr", hidden, dy_proj, preferred_element_type=jnp.float32),
        ],
        1,
    )
    projected_grads = lax.psum(partial_grads, "replica")
    grads_low = projected_grads.astype(jnp.bfloat16)
    mixed = jnp.einsum(
        "sjcf,jfr->sjcr", gate_grad, grads_low[:, 0], preferred_element_type=jnp.float32
    )
    mixed = (
        mixed
        + jnp.einsum("sjcf,jfr->sjcr", up_grad, grads_low[:, 1], preferred_element_type=jnp.float32)
    ).astype(jnp.bfloat16)
    down_mix = jnp.einsum(
        "sjcf,jfr->sjcr", hidden, grads_low[:, 2], preferred_element_type=jnp.float32
    ).astype(jnp.bfloat16)
    power = jnp.einsum("sjcd,sjcr->dr", x_rows, mixed, preferred_element_type=jnp.float32)
    power = power + jnp.einsum(
        "sjcd,sjcr->dr", dy_rows, down_mix, preferred_element_type=jnp.float32
    )
    panel_rows = model_width // group_count
    power_sum = lax.psum(power, ("expert", "replica"))
    gram_total = jnp.dot(
        power_sum.T, power_sum, precision=lax.Precision.HIGHEST, preferred_element_type=jnp.float32
    )
    own_panel = lax.dynamic_slice_in_dim(
        power_sum, lax.axis_index("expert") * panel_rows, panel_rows, 0
    )
    lower = jnp.linalg.cholesky(gram_total)
    new_basis = (
        math.sqrt(model_width) * jax.scipy.linalg.solve_triangular(lower, own_panel.T, lower=True).T
    )
    return (token_grads, projected_grads, new_basis)


def solution(mesh):
    return jax.shard_map(
        body,
        mesh=mesh,
        in_specs=(
            P(("expert", "replica"), None),
            P(("expert", "replica"), None),
            P(("expert", "replica"), None),
            P(("expert", "replica"), None),
            P(("expert", "replica"), None),
            P(("expert", "replica"), None),
            P("expert", None, None),
            P("expert", None, None),
            P("expert", None, None),
            P("expert", None),
        ),
        out_specs=(
            P(("expert", "replica"), None),
            P("expert", None, None, None),
            P("expert", None),
        ),
        check_vma=False,
    )
```

profile of v0, /device:TPU:0, one launch (start us, length us, event | category | flops | bytes accessed | tf_op | source)
XLA Modules:
  0.0 595.4 jit_solution(13270312014699253039)
XLA Ops:
  15.4 10.0 %gather_fusion = bf16[1024,2048]{1,0:T(8,128)(2,1)} fusion(bf16[129,2048]{1,0:T(8,128)(2,1)} %concatenate.15, s32[1024]{0:T(1024)S(1)} %get-tuple-element.37), kind=kCustom, calls=%fused_computation | custom fusion | bytes 8392704 | tf_op jit(solution)/shard_map/gather | solution.py:39
  25.4 6.1 %gather_fusion.1 = f32[1024]{0:T(1024)S(1)} fusion(f32[1025]{0:T(1024)S(1)} %pad_maximum_fusion.1, s32[1024]{0:T(1024)S(1)} %get-tuple-element.36), kind=kCustom, calls=%fused_computation.1 | custom fusion | bytes 12288 | tf_op jit(solution)/shard_map/gather | solution.py:39
  31.5 4.9 fusion
  36.4 7.3 %all-to-all-start = ((bf16[8,128,2048]{2,1,0:T(8,128)(2,1)}), bf16[8,128,2048]{2,1,0:T(8,128)(2,1)}, u32[]{:S(2)}, u32[]{:S(2)}) async-start(bf16[8,128,2048]{2,1,0:T(8,128)(2,1)} %fusion), calls=%async_computation | async-start | bytes 8388608 | tf_op jit(solution)/shard_map/all_to_all | solution.py:50
  45.6 10.0 %gather_fusion.2 = bf16[1024,2048]{1,0:T(8,128)(2,1)} fusion(bf16[129,2048]{1,0:T(8,128)(2,1)} %concatenate.17, s32[1024]{0:T(1024)S(1)} %get-tuple-element.37), kind=kCustom, calls=%fused_computation.2 | custom fusion | bytes 8392704 | tf_op jit(solution)/shard_map/gather | solution.py:38
  55.6 81.4 %all-to-all-done = bf16[8,128,2048]{2,1,0:T(8,128)(2,1)} async-done(((bf16[8,128,2048]{2,1,0:T(8,128)(2,1)}), bf16[8,128,2048]{2,1,0:T(8,128)(2,1)}, u32[]{:S(2)}, u32[]{:S(2)}) %all-to-all-start) | async-done | bytes 4194336 | tf_op jit(solution)/shard_map/all_to_all | solution.py:50
  137.0 4.7 all-to-all-start.1
  143.0 6.6 %fusion.12 = f32[2,8,64,384]{3,2,1,0:T(8,128)} fusion(bf16[8,2,64,2048]{3,2,1,0:T(8,128)(2,1)} %bitcast.3, bf16[2,384,2048]{2,1,0:T(8,128)(2,1)} %param.18), kind=kOutput, calls=%fused_computation.22 | convolution fusion | flops 1610612736 | bytes 8912896 | tf_op jit(solution)/shard_map/sjcd,jfd->sjcf/dot_general | solution.py:71
  149.6 97.3 %all-to-all-done.1 = bf16[8,128,2048]{2,1,0:T(8,128)(2,1)} async-done(((bf16[8,128,2048]{2,1,0:T(8,128)(2,1)}), bf16[8,128,2048]{2,1,0:T(8,128)(2,1)}, u32[]{:S(2)}, u32[]{:S(2)}) %all-to-all-start.1) | async-done | bytes 4194336 | tf_op jit(solution)/shard_map/all_to_all | solution.py:49
  246.9 5.6 fusion.4
  252.6 6.3 %fusion.36 = (bf16[8,2,64,384]{3,2,0,1:T(8,128)(2,1)}, bf16[8,2,64,384]{3,2,0,1:T(8,128)(2,1)S(1)}, bf16[8,2,64,384]{3,2,0,1:T(8,128)(2,1)}) fusion(f32[2,8,64,384]{3,2,1,0:T(8,128)S(1)} %fusion.4, f32[2,8,64,384]{3,2,1,0:T(8,128)S(1)} %copy-done.13, bf16[2,2048,384]{2,1,0:T(8,128)(2,1)S(1)} %copy-done, bf16[8,2,64,2048]{3,2,1,0:T(8,128)(2,1)} %bitcast.8), kind=kOutput, calls=%fused_computation.47 | convolution fusion | flops 1616510976 | bytes 12845056 | tf_op jit(solution)/shard_map/sjcd,jdf->sjcf/dot_general | solution.py:54
  259.8 5.6 fusion.14
  289.4 56.9 %all-reduce.7.cloned.1.call-done = f32[2,3,384,256]{3,2,0,1:T(8,128)} async-done(((f32[2,3,384,256]{3,2,0,1:T(8,128)}), f32[2,3,384,256]{3,2,0,1:T(8,128)}) %all-reduce.7.cloned.1.call-update) | async-done | bytes 2359312 | tf_op jit(solution)/shard_map/psum | solution.py:103
  349.6 5.4 fusion.20
  355.0 6.4 %fusion.26 = f32[2048,256]{1,0:T(8,128)} fusion(f32[2048,256]{1,0:T(8,128)} %fusion.20, bf16[8,2,64,2048]{3,2,1,0:T(8,128)(2,1)} %bitcast.8, f32[2,256,8,64]{1,3,2,0:T(8,128)} %fusion.52, bf16[8,2,64,384]{3,2,0,1:T(8,128)(2,1)S(1)} %copy-done.9, bf16[2,3,384,256]{3,2,0,1:T(8,128)(2,1)} %copy-done.7), kind=kOutput, calls=%fused_computation.32 | convolution fusion | flops 1276116992 | bytes 10616832 | tf_op jit(solution)/shard_map/sjcd,sjcr->dr/dot_general | solution.py:115
  363.2 134.4 %all-reduce.9.cloned.1.call-done = f32[2048,256]{1,0:T(8,128)} async-done(((f32[2048,256]{1,0:T(8,128)}), f32[2048,256]{1,0:T(8,128)}) %all-reduce.9.cloned.1.call-update) | async-done | bytes 2097168 | tf_op jit(solution)/shard_map/psum | solution.py:120
  497.6 5.7 fusion.72
  503.5 11.7 %cholesky.50 = f32[128,128]{1,0:T(8,128)S(1)} custom-call(f32[128,128]{1,0:T(8,128)S(1)} %cholesky.118), custom_call_target="Cholesky" | custom-call | tf_op jit(solution)/shard_map/jit(cholesky)/cholesky | solution.py:127
  515.3 10.0 %custom-call.15 = f32[1,128,128]{1,2,0:T(8,128)S(1)} custom-call(f32[1,128,128]{2,1,0:T(8,128)S(1)} %get-tuple-element.33), custom_call_target="InvertDiagBlocksLowerTriangular" | custom-call | tf_op jit(solution)/shard_map/jit(cholesky)/cholesky | solution.py:127
  525.8 11.7 %cholesky.105 = f32[128,128]{1,0:T(8,128)S(1)} custom-call(f32[128,128]{1,0:T(8,128)S(1)} %convolution_subtract_fusion.1), custom_call_target="Cholesky" | custom-call | tf_op jit(solution)/shard_map/jit(cholesky)/cholesky | solution.py:127
  543.7 19.7 %custom-call.16 = f32[2,128,128]{1,2,0:T(8,128)S(1)} custom-call(f32[2,128,128]{2,1,0:T(8,128)S(1)} %get-tuple-element.10), custom_call_target="InvertDiagBlocksLowerTriangular" | custom-call | tf_op jit(solution)/shard_map/jit(_solve_triangular)/triangular_solve | solution.py:129
  566.3 4.8 concatenate.18
  571.1 11.7 %gather_fusion.3 = bf16[1024,2048]{1,0:T(8,128)(2,1)} fusion(bf16[1025,2048]{1,0:T(8,128)(2,1)} %concatenate.18, s32[1024]{0:T(1024)S(1)} %broadcast_clamp_fusion), kind=kCustom, calls=%fused_computation.3 | custom fusion | bytes 8392704 | tf_op jit(solution)/shard_map/gather | solution.py:90
  582.8 5.9 bitcast_reduce_fusion
  (89 shorter events, 53.6 us)
Async XLA Ops:
  7.2 245.4 %copy-start = (bf16[2,2048,384]{2,1,0:T(8,128)(2,1)S(1)}, bf16[2,2048,384]{2,1,0:T(8,128)(2,1)}, u32[]{:S(2)}) copy-start(bf16[2,2048,384]{2,1,0:T(8,128)(2,1)} %param.17) | copy-start | bytes 9437188
  36.4 100.6 %all-to-all-start = ((bf16[8,128,2048]{2,1,0:T(8,128)(2,1)}), bf16[8,128,2048]{2,1,0:T(8,128)(2,1)}, u32[]{:S(2)}, u32[]{:S(2)}) async-start(bf16[8,128,2048]{2,1,0:T(8,128)(2,1)} %fusion), calls=%async_computation | async-start | bytes 8388608 | tf_op jit(solution)/shard_map/all_to_all | solution.py:50
  137.0 5.2 copy-start.12
  137.0 109.9 %all-to-all-start.1 = ((bf16[8,128,2048]{2,1,0:T(8,128)(2,1)}), bf16[8,128,2048]{2,1,0:T(8,128)(2,1)}, u32[]{:S(2)}, u32[]{:S(2)}) async-start(bf16[8,128,2048]{2,1,0:T(8,128)(2,1)} %bitcast.178), calls=%async_computation.1 | async-start | bytes 8388608 | tf_op jit(solution)/shard_map/all_to_all | solution.py:49
  141.7 123.7 %all-gather.2.cloned.1.call-start = ((), (), s32[]{:S(2)}) async-start(), calls=%async_computation.3 | async-start | bytes 1179648 | tf_op jit(solution)/shard_map/all_gather | solution.py:43
  246.9 5.6 copy-start.13
  252.6 7.2 %copy-start.6 = (bf16[2,2048,384]{2,1,0:T(8,128)(2,1)S(1)}, bf16[2,2048,384]{2,1,0:T(8,128)(2,1)}, u32[]{:S(2)}) copy-start(bf16[2,2048,384]{2,1,0:T(8,128)(2,1)} %param.16) | copy-start | bytes 9437188
  258.9 0.9 copy-start.4
  265.4 6.6 %copy-start.8 = (bf16[8,2,64,384]{3,2,0,1:T(8,128)(2,1)S(1)}, bf16[8,2,64,384]{3,2,0,1:T(8,128)(2,1)}, u32[]{:S(2)}) copy-start(bf16[8,2,64,384]{3,2,0,1:T(8,128)(2,1)} %get-tuple-element.29) | copy-start | bytes 2359300
  265.4 8.0 %copy-start.2 = (f32[2,8,64,2048]{3,2,1,0:T(8,128)S(1)}, f32[2,8,64,2048]{3,2,1,0:T(8,128)}, u32[]{:S(2)}) copy-start(f32[2,8,64,2048]{3,2,1,0:T(8,128)} %fusion.14) | copy-start | bytes 25165828
  278.3 4.7 copy-start.14
  278.3 288.0 %all-to-all-start.2 = ((bf16[8,128,2048]{2,1,0:T(8,128)(2,1)}), bf16[8,128,2048]{2,1,0:T(8,128)(2,1)}, u32[]{:S(2)}, u32[]{:S(2)}) async-start(bf16[8,128,2048]{2,1,0:T(8,128)(2,1)} %bitcast.180), calls=%async_computation.2 | async-start | bytes 8388608 | tf_op jit(solution)/shard_map/all_to_all | solution.py:85
  283.0 63.4 %all-reduce.7.cloned.1.call-start = ((), (), s32[]{:S(2)}) async-start(), calls=%async_computation.4 | async-start | bytes 4718592 | tf_op jit(solution)/shard_map/psum | solution.py:103
  283.0 4.4 copy-start.10
  283.1 4.4 copy-start.11
  289.2 59.0 %copy-start.5 = (bf16[8,2,64,384]{3,2,0,1:T(8,128)(2,1)S(1)}, bf16[8,2,64,384]{3,2,0,1:T(8,128)(2,1)}, u32[]{:S(2)}) copy-start(bf16[8,2,64,384]{3,2,0,1:T(8,128)(2,1)} %copy-done.4) | copy-start | bytes 2359300
  289.2 208.4 %all-reduce.9.cloned.1.call-start = ((), (), s32[]{:S(2)}) async-start(), calls=%async_computation.5 | async-start | bytes 4194304 | tf_op jit(solution)/shard_map/psum | solution.py:120
  348.2 1.5 copy-start.7
  349.6 5.4 copy-start.9
  355.0 6.5 %copy-start.3 = (f32[2,3,384,256]{3,2,0,1:T(8,128)S(1)}, f32[2,3,384,256]{3,2,0,1:T(8,128)}, u32[]{:S(2)}) copy-start(f32[2,3,384,256]{3,2,0,1:T(8,128)} %all-reduce.7.cloned.1.call-done) | copy-start | bytes 7077892
  571.1 17.6 %copy-start.1 = (bf16[2,2048,384]{2,1,0:T(8,128)(2,1)S(1)}, bf16[2,2048,384]{2,1,0:T(8,128)(2,1)}, u32[]{:S(2)}) copy-start(bf16[2,2048,384]{2,1,0:T(8,128)(2,1)} %param.17) | copy-start | bytes 9437188
Sparse Core Ops, SparseCore 0:
  145.2 102.1 all-gather.1
  289.3 56.9 all-reduce.6
  361.6 135.9 all-reduce.8
where the time goes:
time: 600 us; the launch traced here: 595 us
  waiting for transfers between devices  370 us (62%)
  other arithmetic  69.8 us (12%)
  local copies, waits for them, and re-layouts  63 us (10%)
  matrix products  59.4 us (10%)
  starting transfers between devices  17.4 us (3%)
  between operations  15.7 us (3%)
    psum x1, waiting for transfers between devices, body(): power_sum = lax.psum(power, ('expert', 'replica'))  134 us
    all_to_all x1, waiting for transfers between devices, body(): lax.all_to_all(x_send, 'expert', split_axis=0, concat_axis=0, tiled=True)  97.3 us
    all_to_all x1, waiting for transfers between devices, body(): lax.all_to_all(dy_send, 'expert', split_axis=0, concat_axis=0, tiled=True)  81.4 us
    psum x1, waiting for transfers between devices, body(): projected_grads = lax.psum(partial_grads, 'replica')  56.9 us
    another operation x6, other arithmetic, body(): lower = jnp.linalg.cholesky(gram_total)  34.2 us
    another operation x3, other arithmetic, body(): jax.scipy.linalg.solve_triangular(lower, own_panel.T, lower=True)  19.7 us
  transfers between devices with their start and end apart: 6, of which 4 were waited for; matrix products, arithmetic and copies ran while one was open for 21% of the time, Pallas kernels for 0%

commit v1 on v0

--- a/solution.py
+++ b/solution.py
@@ -117,7 +117,7 @@
         "sjcd,sjcr->dr", dy_rows, down_mix, preferred_element_type=jnp.float32
     )
     panel_rows = model_width // group_count
-    power_sum = lax.psum(power, ("expert", "replica"))
+    power_sum = jnp.sum(lax.all_gather(power, ("expert", "replica")), axis=0)
     gram_total = jnp.dot(
         power_sum.T, power_sum, precision=lax.Precision.HIGHEST, preferred_element_type=jnp.float32
     )

time: 600 us -> 883 us (1.47)
  waiting for transfers between devices: 370 us -> 617 us
  other arithmetic: 69.8 us -> 97.6 us
    all_gather x0 -> x1, waiting for transfers between devices: none -> 204 us  [body(): power_sum = jnp.sum(lax.all_gather(power, ('expert', 'replica')), axis=0)]
    all_to_all x1, waiting for transfers between devices: 0.01 us -> 191 us  [body(): lax.all_to_all(row_grads, 'expert', split_axis=0, concat_axis=0, tiled=True)]
    psum x1 -> x0, waiting for transfers between devices: 134 us -> none  [body(): power_sum = lax.psum(power, ('expert', 'replica'))]
    all_to_all x1, waiting for transfers between devices: 97.3 us -> 70.1 us  [body(): lax.all_to_all(x_send, 'expert', split_axis=0, concat_axis=0, tiled=True)]
    reduce_sum x0 -> x1, other arithmetic: none -> 22.4 us  [body(): power_sum = jnp.sum(lax.all_gather(power, ('expert', 'replica')), axis=0)]
    all_to_all x1, waiting for transfers between devices: 81.4 us -> 97.3 us  [body(): lax.all_to_all(dy_send, 'expert', split_axis=0, concat_axis=0, tiled=True)]
  transfers between devices with their start and end apart: 6 -> 6, of which waited for: 4 -> 5; matrix products, arithmetic and copies ran while one was open for 21% -> 9% of each run, Pallas kernels for 0% -> 0%
where the time goes in v1:
time: 883 us; the launch traced here: 878 us
  waiting for transfers between devices  617 us (70%)
  other arithmetic  97.6 us (11%)
  local copies, waits for them, and re-layouts  66.6 us (8%)
  matrix products  62.8 us (7%)
  starting transfers between devices  18.2 us (2%)
  between operations  15.5 us (2%)
    all_gather x1, waiting for transfers between devices, body(): power_sum = jnp.sum(lax.all_gather(power, ('expert', 'replica')), axis=0)  204 us
    all_to_all x1, waiting for transfers between devices, body(): lax.all_to_all(row_grads, 'expert', split_axis=0, concat_axis=0, tiled=True)  191 us
    all_to_all x1, waiting for transfers between devices, body(): lax.all_to_all(dy_send, 'expert', split_axis=0, concat_axis=0, tiled=True)  97.3 us
    all_to_all x1, waiting for transfers between devices, body(): lax.all_to_all(x_send, 'expert', split_axis=0, concat_axis=0, tiled=True)  70.1 us
    psum x1, waiting for transfers between devices, body(): projected_grads = lax.psum(partial_grads, 'replica')  54.6 us
    another operation x6, other arithmetic, body(): lower = jnp.linalg.cholesky(gram_total)  34.2 us
    reduce_sum x1, other arithmetic, body(): power_sum = jnp.sum(lax.all_gather(power, ('expert', 'replica')), axis=0)  22.4 us
    another operation x3, other arithmetic, body(): jax.scipy.linalg.solve_triangular(lower, own_panel.T, lower=True)  21.5 us
  transfers between devices with their start and end apart: 6, of which 5 were waited for; matrix products, arithmetic and copies ran while one was open for 9% of the time, Pallas kernels for 0%

profile of v1, /device:TPU:0, one launch (start us, length us, event | category | flops | bytes accessed | tf_op | source)
XLA Modules:
  0.0 878.0 jit_solution(3629382021930836518)
XLA Ops:
  14.5 10.0 %gather_fusion.2 = bf16[1024,2048]{1,0:T(8,128)(2,1)} fusion(bf16[129,2048]{1,0:T(8,128)(2,1)} %concatenate.17, s32[1024]{0:T(1024)S(1)} %get-tuple-element.37), kind=kCustom, calls=%fused_computation.2 | custom fusion | bytes 8392704 | tf_op jit(solution)/shard_map/gather | solution.py:38
  24.5 7.3 all-to-all-start.1
  33.7 10.0 %gather_fusion = bf16[1024,2048]{1,0:T(8,128)(2,1)} fusion(bf16[129,2048]{1,0:T(8,128)(2,1)} %concatenate.15, s32[1024]{0:T(1024)S(1)} %get-tuple-element.37), kind=kCustom, calls=%fused_computation | custom fusion | bytes 8392704 | tf_op jit(solution)/shard_map/gather | solution.py:39
  43.9 6.2 gather_fusion.1
  54.9 70.1 %all-to-all-done.1 = bf16[8,128,2048]{2,1,0:T(8,128)(2,1)} async-done(((bf16[8,128,2048]{2,1,0:T(8,128)(2,1)}), bf16[8,128,2048]{2,1,0:T(8,128)(2,1)}, u32[]{:S(2)}, u32[]{:S(2)}) %all-to-all-start.1) | async-done | bytes 4194336 | tf_op jit(solution)/shard_map/all_to_all | solution.py:49
  131.0 6.6 fusion.4
  137.6 97.3 %all-to-all-done = bf16[8,128,2048]{2,1,0:T(8,128)(2,1)} async-done(((bf16[8,128,2048]{2,1,0:T(8,128)(2,1)}), bf16[8,128,2048]{2,1,0:T(8,128)(2,1)}, u32[]{:S(2)}, u32[]{:S(2)}) %all-to-all-start) | async-done | bytes 4194336 | tf_op jit(solution)/shard_map/all_to_all | solution.py:50
  234.9 5.6 fusion.12
  240.5 6.4 fusion.36
  253.5 5.5 convolution_bitcast_fusion
  262.4 54.6 %all-reduce.6.cloned.1.call-done = f32[2,3,384,256]{3,2,0,1:T(8,128)} async-done(((f32[2,3,384,256]{3,2,0,1:T(8,128)}), f32[2,3,384,256]{3,2,0,1:T(8,128)}) %all-reduce.6.cloned.1.call-update) | async-done | bytes 2359312 | tf_op jit(solution)/shard_map/psum | solution.py:103
  319.9 5.4 fusion.20
  328.0 6.5 fusion.26
  344.4 5.5 all-to-all-start.2
  353.3 191.2 %all-to-all-done.2 = bf16[8,128,2048]{2,1,0:T(8,128)(2,1)} async-done(((bf16[8,128,2048]{2,1,0:T(8,128)(2,1)}), bf16[8,128,2048]{2,1,0:T(8,128)(2,1)}, u32[]{:S(2)}, u32[]{:S(2)}) %all-to-all-start.2) | async-done | bytes 4194336 | tf_op jit(solution)/shard_map/all_to_all | solution.py:85
  549.3 11.6 %gather_fusion.3 = bf16[1024,2048]{1,0:T(8,128)(2,1)} fusion(bf16[1025,2048]{1,0:T(8,128)(2,1)} %concatenate.18, s32[1024]{0:T(1024)S(1)} %broadcast_clamp_fusion), kind=kCustom, calls=%fused_computation.3 | custom fusion | bytes 8392704 | tf_op jit(solution)/shard_map/gather | solution.py:90
  560.9 5.9 bitcast_reduce_fusion
  566.8 203.9 %all-gather.6.cloned.1.call-done = f32[65536,256]{1,0:T(8,128)} async-done(((f32[2048,256]{1,0:T(8,128)}), f32[65536,256]{1,0:T(8,128)}) %all-gather.6.cloned.1.call-update) | async-done | bytes 67108880 | tf_op jit(solution)/shard_map/all_gather | solution.py:120
  770.8 22.4 %reduce_sum.22 = f32[2048,256]{1,0:T(8,128)} reduce(f32[32,2048,256]{2,1,0:T(8,128)} %bitcast.47, f32[]{:T(128)} %constant.119.clone.1), dimensions={0}, to_apply=%region_3.4 | reduce | flops 16252928 | bytes 69206016 | tf_op jit(solution)/shard_map/reduce_sum | solution.py:120
  793.1 5.7 fusion.72
  801.4 11.7 %cholesky.50 = f32[128,128]{1,0:T(8,128)S(1)} custom-call(f32[128,128]{1,0:T(8,128)S(1)} %cholesky.118), custom_call_target="Cholesky" | custom-call | tf_op jit(solution)/shard_map/jit(cholesky)/cholesky | solution.py:127
  814.8 9.8 %custom-call.15 = f32[1,128,128]{1,2,0:T(8,128)S(1)} custom-call(f32[1,128,128]{2,1,0:T(8,128)S(1)} %get-tuple-element.33), custom_call_target="InvertDiagBlocksLowerTriangular" | custom-call | tf_op jit(solution)/shard_map/jit(cholesky)/cholesky | solution.py:127
  826.8 12.0 %cholesky.105 = f32[128,128]{1,0:T(8,128)S(1)} custom-call(f32[128,128]{1,0:T(8,128)S(1)} %convolution_subtract_fusion.1), custom_call_target="Cholesky" | custom-call | tf_op jit(solution)/shard_map/jit(cholesky)/cholesky | solution.py:127
  847.0 20.5 %custom-call.16 = f32[2,128,128]{1,2,0:T(8,128)S(1)} custom-call(f32[2,128,128]{2,1,0:T(8,128)} %get-tuple-element.10), custom_call_target="InvertDiagBlocksLowerTriangular" | custom-call | tf_op jit(solution)/shard_map/jit(_solve_triangular)/triangular_solve | solution.py:129
  (78 shorter events, 76.1 us)
Async XLA Ops:
  7.2 233.4 %copy-start = (bf16[2,2048,384]{2,1,0:T(8,128)(2,1)S(1)}, bf16[2,2048,384]{2,1,0:T(8,128)(2,1)}, u32[]{:S(2)}) copy-start(bf16[2,2048,384]{2,1,0:T(8,128)(2,1)} %param.17) | copy-start | bytes 9437188
  24.5 100.6 %all-to-all-start.1 = ((bf16[8,128,2048]{2,1,0:T(8,128)(2,1)}), bf16[8,128,2048]{2,1,0:T(8,128)(2,1)}, u32[]{:S(2)}, u32[]{:S(2)}) async-start(bf16[8,128,2048]{2,1,0:T(8,128)(2,1)} %bitcast.179), calls=%async_computation.1 | async-start | bytes 8388608 | tf_op jit(solution)/shard_map/all_to_all | solution.py:49
  33.7 10.0 %copy-start.7 = (f32[128,8]{0,1:T(8,128)S(1)}, f32[128,8]{0,1:T(8,128)}, u32[]{:S(2)}) copy-start(f32[128,8]{0,1:T(8,128)} %param.12) | copy-start | bytes 12292
  54.9 74.8 %copy-start.6 = (f32[256,256]{1,0:T(8,128)S(1)}, f32[256,256]{1,0:T(8,128)}, u32[]{:S(2)}) copy-start(f32[256,256]{1,0:T(8,128)} %param.19) | copy-start | bytes 786436
  125.1 109.8 %all-to-all-start = ((bf16[8,128,2048]{2,1,0:T(8,128)(2,1)}), bf16[8,128,2048]{2,1,0:T(8,128)(2,1)}, u32[]{:S(2)}, u32[]{:S(2)}) async-start(bf16[8,128,2048]{2,1,0:T(8,128)(2,1)} %fusion), calls=%async_computation | async-start | bytes 8388608 | tf_op jit(solution)/shard_map/all_to_all | solution.py:50
  129.7 117.3 %all-gather.4.cloned.1.call-start = ((), (), s32[]{:S(2)}) async-start(), calls=%async_computation.3 | async-start | bytes 1179648 | tf_op jit(solution)/shard_map/all_gather | solution.py:43
  130.4 186.6 %all-reduce.6.cloned.1.call-start = ((), (), s32[]{:S(2)}) async-start(), calls=%async_computation.4 | async-start | bytes 4718592 | tf_op jit(solution)/shard_map/psum | solution.py:103
  234.9 5.6 copy-start.8
  246.9 3.9 copy-start.4
  246.9 5.2 copy-start.1
  262.2 508.5 %all-gather.6.cloned.1.call-start = ((), (), s32[]{:S(2)}) async-start(), calls=%async_computation.5 | async-start | bytes 69206016 | tf_op jit(solution)/shard_map/all_gather | solution.py:120
  334.5 4.6 copy-start.5
  344.4 200.1 %all-to-all-start.2 = ((bf16[8,128,2048]{2,1,0:T(8,128)(2,1)}), bf16[8,128,2048]{2,1,0:T(8,128)(2,1)}, u32[]{:S(2)}, u32[]{:S(2)}) async-start(bf16[8,128,2048]{2,1,0:T(8,128)(2,1)} %bitcast.181), calls=%async_computation.2 | async-start | bytes 8388608 | tf_op jit(solution)/shard_map/all_to_all | solution.py:85
  800.6 0.7 copy-start.3
  838.8 2.0 copy-start.2
Sparse Core Ops, SparseCore 0:
  133.2 102.2 all-gather.3
  262.3 54.6 all-reduce.5
  334.6 436.0 all-gather.5
